TPU v7x, 128 devices: a whole 4x4x4 slice. The times are simulated.
128 devices in a mesh: req: 32 (over y, z, core), tensor: 4 (over x).
Axes of the slice: x: 4, y: 4, z: 4, core: 2. Of those that a mesh axis runs over, the one named last changes fastest.
Arguments:
- hidden: bfloat16 [32768, 1024], P('req', 'tensor')
- gain: bfloat16 [1024], P('tensor'), may hold values from 0.5 to 1.5
- head: bfloat16 [1024, 32128], P(None, ('req', 'tensor'))
- token_ids: int32 [32768], P('req'), may hold values from 0 to 32127
- lengths: int32 [32], P('req'), may hold values from 1 to 1024, 12288 in all
- prompt_of: int32 [32], P('req'), may hold values from 0 to 3, as said below
Outputs:
- token_logprob: float32 [32768], P(('req', 'tensor'))
- token_entropy: float32 [32768], P(('req', 'tensor'))
- prompt_stats: float32 [4, 2], replicated
Inputs may be any that keep to these rules, and one draw needn't show every extreme that they name: The lengths sum to 12288 and the longest is exactly 1024. `prompt_of`: a prompt may have no responses.
All inputs are finite; a program needn't handle non-finite values. No bound on the sum of `lengths` on one device may be relied on, other than what follows from the above.
Results may differ from a plain program's by a relative error of at most 0.0019.
Values may be sent and summed in bfloat16 or wider, within the bound.
A program may use at most 128 MiB of HBM per device.

v0:
```python
import jax
import jax.numpy as jnp
from jax import lax
from jax.sharding import PartitionSpec as P

PROMPTS = 4
NEG = -1e30
eps = 1e-06


def chunk_stats(normed, piece, vocab_ids, valid, ids):
    logits = lax.dot_general(
        normed, piece, (((1,), (1,)), ((), ())), preferred_element_type=jnp.float32
    )
    logits = jnp.where(valid[None, :], logits, NEG)
    top = jnp.max(logits, axis=1)
    expo = jnp.exp(logits - top[:, None])
    total = jnp.sum(expo, axis=1)
    moment = jnp.sum(expo * logits, axis=1)
    pick = jnp.sum(jnp.where(vocab_ids[None, :] == ids[:, None], logits, 0.0), axis=1)
    return (top, total, moment, pick)


def merge(stats):
    tops = jnp.stack([s[0] for s in stats])
    top = jnp.max(tops, axis=0)
    factor = jnp.exp(tops - top[None, :])
    total = jnp.sum(factor * jnp.stack([s[1] for s in stats]), axis=0)
    moment = jnp.sum(factor * jnp.stack([s[2] for s in stats]), axis=0)
    pick = jnp.sum(jnp.stack([s[3] for s in stats]), axis=0)
    return (top, total, moment, pick)


def local(hidden, gain, head, token_ids, lengths, prompt_of):
    rows, part_width = hidden.shape
    splits = lax.axis_size("tensor")
    column_index = lax.axis_index("tensor")
    req_count = lax.axis_size("req")
    shard_cols = head.shape[1]
    width = part_width * splits
    extra = jnp.zeros((8, part_width), hidden.dtype).at[0].set(gain)
    packed = jnp.concatenate([hidden, extra], axis=0)
    gathered = lax.all_gather(packed, "tensor", axis=1, tiled=True)
    widened = gathered[:rows].astype(jnp.float32)
    gain_full = gathered[rows].astype(jnp.float32)
    scale = lax.rsqrt(jnp.sum(widened * widened, axis=1) / width + eps)
    normed = (widened * scale[:, None] * gain_full[None, :]).astype(jnp.bfloat16)
    head_t = head.T
    chunk = 128
    bounds = [(lo, min(lo + chunk, shard_cols)) for lo in range(0, shard_cols, chunk)]
    stats = []
    for lo, hi in bounds:
        part = head_t[lo:hi]
        if hi - lo < chunk:
            part = jnp.concatenate(
                [part, jnp.zeros((chunk - (hi - lo), part.shape[1]), part.dtype)], axis=0
            )
        piece = lax.all_gather(part, "req", axis=0, tiled=True)
        g = jnp.arange(req_count * chunk, dtype=jnp.int32)
        owner = g // chunk
        offset = lo + g % chunk
        valid = offset < hi
        vocab_ids = jnp.where(valid, (owner * splits + column_index) * shard_cols + offset, -1)
        stats.append(chunk_stats(normed, piece, vocab_ids, valid, token_ids))
    mine = merge(stats)
    everyone = lax.all_gather(jnp.stack(mine), "tensor", axis=0, tiled=False)
    top, total, moment, picked = merge(
        [tuple((everyone[k, j] for j in range(4))) for k in range(splits)]
    )
    positions = jnp.arange(rows, dtype=jnp.int32)
    live = positions < lengths[0]
    safe_total = jnp.where(live, total, 1.0)
    log_norm = top + jnp.log(safe_total)
    logprob = jnp.where(live, picked - log_norm, 0.0)
    entropy = jnp.where(live, log_norm - moment / safe_total, 0.0)
    onehot = (jnp.arange(PROMPTS, dtype=jnp.int32) == prompt_of[0]).astype(jnp.float32)
    summary = jnp.stack([jnp.sum(entropy), jnp.sum(logprob), lengths[0].astype(jnp.float32)])
    summed = lax.psum(onehot[:, None] * summary[None, :], "req")
    prompt_stats = summed[:, :2] / jnp.maximum(summed[:, 2:3], 1.0)
    share = rows // splits
    own_logprob = lax.dynamic_slice_in_dim(logprob, column_index * share, share)
    own_entropy = lax.dynamic_slice_in_dim(entropy, column_index * share, share)
    return (own_logprob, own_entropy, prompt_stats)


def solution(mesh):
    in_specs = (
        P("req", "tensor"),
        P("tensor"),
        P(None, ("req", "tensor")),
        P("req"),
        P("req"),
        P("req"),
    )
    out_specs = (P(("req", "tensor")), P(("req", "tensor")), P())
    return jax.shard_map(local, mesh=mesh, in_specs=in_specs, out_specs=out_specs, check_vma=False)
```

profile of v0, /device:TPU:1, one launch (start us, length us, event | category | flops | bytes accessed | tf_op | source)
XLA Modules:
  0.0 288.1 jit_solution(5569118323441243432)
XLA Ops:
  7.2 0.7 reshape.148
  7.9 1.9 fusion.6
  9.8 0.0 all-gather.8.cloned.1.call-start
  9.8 1.7 slice.104
  11.5 0.0 all-gather.10.cloned.1.call-start
  11.6 1.0 slice.105
  12.6 0.8 concatenate.9
  14.7 31.1 %all-gather.6.cloned.1.call-done = bf16[1032,1024]{1,0:T(8,128)(2,1)} async-done(((bf16[1032,256]{1,0:T(8,128)(2,1)}), bf16[1032,1024]{1,0:T(8,128)(2,1)}) %all-gather.6.cloned.1.call-update) | async-done | bytes 2113552 | tf_op jit(solution)/shard_map/all_gather | solution.py:43
  45.8 2.1 fusion.2
  47.9 0.7 slice_convert_fusion
  48.6 61.1 %all-gather.8.cloned.1.call-done = bf16[4096,1024]{0,1:T(8,128)(2,1)} async-done(((bf16[128,1024]{0,1:T(8,128)(2,1)}), bf16[4096,1024]{0,1:T(8,128)(2,1)}) %all-gather.8.cloned.1.call-update) | async-done | bytes 8388624 | tf_op jit(solution)/shard_map/all_gather | solution.py:58
  109.7 16.5 %select_reduce_fusion.3 = (f32[1024]{0:T(1024)S(1)}, f32[1024,4096]{1,0:T(8,128)}) fusion(pred[4096]{0:T(1024)(128)(4,1)S(1)} %get-tuple-element.53, bf16[4096,1024]{0,1:T(8,128)(2,1)} %all-gather.8.cloned.1.call-done, f32[1024]{0:T(1024)S(1)} %bitcast.69, f32[1024]{0:T(1024)S(1)} %add_rsqrt_fusion, bf16[1032,1024]{1,0:T(8,128)(2,1)} %all-gather.6.cloned.1.call-done), kind=kOutput, calls=%fused_computation.9 | convolution fusion | flops 8602516480 | bytes 27279360 | tf_op jit(solution)/shard_map/dot_general | solution.py:12
  126.2 44.3 %all-gather.10.cloned.1.call-done = bf16[4096,1024]{0,1:T(8,128)(2,1)} async-done(((bf16[128,1024]{0,1:T(8,128)(2,1)}), bf16[4096,1024]{0,1:T(8,128)(2,1)}) %all-gather.10.cloned.1.call-update) | async-done | bytes 8388624 | tf_op jit(solution)/shard_map/all_gather | solution.py:58
  170.5 14.7 %select_reduce_fusion.2 = (f32[1024]{0:T(1024)S(1)}, f32[1024,4096]{1,0:T(8,128)}) fusion(pred[4096]{0:T(1024)(128)(4,1)S(1)} %get-tuple-element.54, bf16[4096,1024]{0,1:T(8,128)(2,1)} %all-gather.10.cloned.1.call-done, f32[1024]{0:T(1024)S(1)} %bitcast.70, f32[1024]{0:T(1024)S(1)} %add_rsqrt_fusion, bf16[1032,1024]{1,0:T(8,128)(2,1)S(1)} %copy-done), kind=kOutput, calls=%fused_computation.8 | convolution fusion | flops 8602516480 | bytes 27279360 | tf_op jit(solution)/shard_map/dot_general | solution.py:12
  185.3 17.7 %fusion = (f32[1024]{0:T(1024)S(1)}, f32[1024]{0:T(1024)S(1)}, f32[1024]{0:T(1024)S(1)}, f32[1024]{0:T(1024)S(1)}, f32[1024]{0:T(1024)S(1)}, /*index=5*/f32[1024]{0:T(1024)S(1)}) fusion(f32[1024,4096]{1,0:T(8,128)} %get-tuple-element.48, f32[1024]{0:T(1024)S(1)} %get-tuple-element.47, pred[4096]{0:T(1024)(128)(4,1)S(1)} %get-tuple-element.54, ...), kind=kLoop, calls=%fused_computation.5 | loop fusion | flops 67102720 | bytes 33632256 | tf_op jit(solution)/shard_map/reduce_sum | solution.py:18
  203.1 9.6 %all-gather.1 = f32[4,4,1024]{2,1,0:T(4,128)S(1)} all-gather(f32[1,4,1024]{2,1,0:T(4,128)S(1)} %maximum_bitcast_fusion), channel_id=2, replica_groups=mesh['req'=32,'tensor'=4] {'tensor'}, dimensions={0}, use_global_device_ids=true | all-gather | bytes 81920 | tf_op jit(solution)/shard_map/all_gather | solution.py:66
  212.7 0.1 fusion.21
  212.8 0.6 fusion.33
  213.4 1.4 pad_maximum_fusion
  214.8 0.1 broadcast_multiply_fusion
  214.9 64.9 %psum.7 = f32[4,3]{0,1:T(4,128)S(1)} all-reduce(f32[4,3]{0,1:T(4,128)S(1)} %broadcast_multiply_fusion), channel_id=1, replica_groups=mesh['req'=32,'tensor'=4] {'req'}, use_global_device_ids=true, to_apply=%region_15.16 | all-reduce | flops 12 | bytes 96 | tf_op jit(solution)/shard_map/psum | solution.py:78
  279.7 0.6 slice_divide_fusion
  280.3 0.6 dynamic_slice.7
  281.0 0.6 dynamic_slice.6
  (29 shorter events, 0.3 us)
Async XLA Ops:
  7.2 38.7 %all-gather.6.cloned.1.call-start = ((), (), s32[]{:S(2)}) async-start(), calls=%async_computation | async-start | bytes 2641920 | tf_op jit(solution)/shard_map/all_gather | solution.py:43
  9.8 99.9 %all-gather.8.cloned.1.call-start = ((), (), s32[]{:S(2)}) async-start(), calls=%async_computation.1 | async-start | bytes 8650752 | tf_op jit(solution)/shard_map/all_gather | solution.py:58
  11.5 158.9 %all-gather.10.cloned.1.call-start = ((), (), s32[]{:S(2)}) async-start(), calls=%async_computation.2 | async-start | bytes 8650752 | tf_op jit(solution)/shard_map/all_gather | solution.py:58
  109.7 60.8 %copy-start = (bf16[1032,1024]{1,0:T(8,128)(2,1)S(1)}, bf16[1032,1024]{1,0:T(8,128)(2,1)}, u32[]{:S(2)}) copy-start(bf16[1032,1024]{1,0:T(8,128)(2,1)} %all-gather.6.cloned.1.call-done) | copy-start | bytes 6340612
  170.5 14.8 %slice-start = ((s8[16777216]{0:T(1024)(128)(4,1)}), s8[4194304]{0:T(1024)(128)(4,1)S(1)}, s32[]{:S(2)}) async-start(s8[16777216]{0:T(1024)(128)(4,1)} %bitcast.51), calls=%async_computation.3 | async-start | bytes 8388608
  170.5 14.8 %slice-start.1 = ((s8[16777216]{0:T(1024)(128)(4,1)}), s8[4194304]{0:T(1024)(128)(4,1)S(1)}, s32[]{:S(2)}) async-start(s8[16777216]{0:T(1024)(128)(4,1)} %bitcast.51), calls=%async_computation.4 | async-start | bytes 8388608
  170.5 14.8 %slice-start.2 = ((s8[16777216]{0:T(1024)(128)(4,1)}), s8[4194304]{0:T(1024)(128)(4,1)S(1)}, s32[]{:S(2)}) async-start(s8[16777216]{0:T(1024)(128)(4,1)} %bitcast.51), calls=%async_computation.5 | async-start | bytes 8388608
  170.5 14.8 %slice-start.3 = ((s8[16777216]{0:T(1024)(128)(4,1)}), s8[4194304]{0:T(1024)(128)(4,1)S(1)}, s32[]{:S(2)}) async-start(s8[16777216]{0:T(1024)(128)(4,1)} %bitcast.51), calls=%async_computation.6 | async-start | bytes 8388608
  170.5 14.8 %copy-start.1 = (s32[1024]{0:T(1024)S(1)}, s32[1024]{0:T(1024)}, u32[]{:S(2)}) copy-start(s32[1024]{0:T(1024)} %param.11) | copy-start | bytes 12292
Sparse Core Ops, SparseCore 0:
  9.9 35.8 all-gather.5
  48.0 61.6 all-gather.7
  111.9 58.5 all-gather.9
where the time goes:
time: 288 us
  waiting for transfers between devices  137 us (48%)
  blocking collectives  74.4 us (26%)
  matrix products  31.2 us (11%)
  other arithmetic  25.2 us (9%)
  between operations  15.2 us (5%)
  local copies, waits for them, and re-layouts  5.38 us (2%)
    all_gather x2, waiting for transfers between devices, local(): piece = lax.all_gather(part, 'req', axis=0, tiled=True)  105 us
    psum x1, blocking collectives, local(): summed = lax.psum(onehot[:, None] * summary[None, :], 'req')  64.9 us
    dot_general x2, matrix products, chunk_stats(): lax.dot_general(normed, piece, (((1,), (1,)), ((), ())), preferred_elemen...  31.2 us
    all_gather x1, waiting for transfers between devices, local(): gathered = lax.all_gather(packed, 'tensor', axis=1, tiled=True)  31.1 us
    reduce_sum x1, other arithmetic, chunk_stats(): total = jnp.sum(expo, axis=1)  17.7 us
    all_gather x1, blocking collectives, local(): everyone = lax.all_gather(jnp.stack(mine), 'tensor', axis=0, tiled=False)  9.59 us
  transfers between devices with their start and end apart: 3, of which 3 were waited for; matrix products, arithmetic and copies ran while one was open for 8% of the time, Pallas kernels for 0%

commit v1 on v0

--- a/solution.py
+++ b/solution.py
@@ -40,7 +40,24 @@
     width = part_width * splits
     extra = jnp.zeros((8, part_width), hidden.dtype).at[0].set(gain)
     packed = jnp.concatenate([hidden, extra], axis=0)
-    gathered = lax.all_gather(packed, "tensor", axis=1, tiled=True)
+    size, place, rows_2 = (lax.axis_size("tensor"), lax.axis_index("tensor"), packed.shape[1])
+    right = [(i, (i + 1) % size) for i in range(size)]
+    downward = [(i, (i - 1) % size) for i in range(size)]
+    result = jnp.zeros((*packed.shape[:1], size * rows_2, *packed.shape[1 + 1 :]), packed.dtype)
+    result = lax.dynamic_update_slice_in_dim(result, packed, place * rows_2, axis=1)
+    from_left = from_right = packed
+    middle = size // 2
+    for turn in range(1, middle + 1):
+        from_left = lax.ppermute(from_left, "tensor", right)
+        result = lax.dynamic_update_slice_in_dim(
+            result, from_left, (place - turn) % size * rows_2, axis=1
+        )
+        if turn < size - middle:
+            from_right = lax.ppermute(from_right, "tensor", downward)
+            result = lax.dynamic_update_slice_in_dim(
+                result, from_right, (place + turn) % size * rows_2, axis=1
+            )
+    gathered = result
     widened = gathered[:rows].astype(jnp.float32)
     gain_full = gathered[rows].astype(jnp.float32)
     scale = lax.rsqrt(jnp.sum(widened * widened, axis=1) / width + eps)

time: 288 us -> 252 us (0.88)
  waiting for transfers between devices: 137 us -> 99.1 us
  starting transfers between devices: 0.12 us -> 3.91 us
  other arithmetic: 25.2 us -> 21.5 us
    all_gather x1 -> x0, waiting for transfers between devices: 31.1 us -> none  [local(): gathered = lax.all_gather(packed, 'tensor', axis=1, tiled=True)]
    all_gather x2, waiting for transfers between devices: 105 us -> 77.5 us  [local(): piece = lax.all_gather(part, 'req', axis=0, tiled=True)]
    ppermute x0 -> x3, waiting for transfers between devices: none -> 21.6 us  [the longest x2 21.6 us: local(): from_left = lax.ppermute(from_left, 'tensor', right)]
    ppermute x0 -> x3, starting transfers between devices: none -> 3.83 us  [the longest x2 2.48 us: local(): from_left = lax.ppermute(from_left, 'tensor', right)]
  transfers between devices with their start and end apart: 3 -> 5, of which waited for: 3 -> 4; matrix products, arithmetic and copies ran while one was open for 8% -> 8% of each run, Pallas kernels for 0% -> 0%
where the time goes in v1:
time: 252 us
  waiting for transfers between devices  99.1 us (39%)
  blocking collectives  74.4 us (30%)
  matrix products  29.3 us (12%)
  other arithmetic  21.5 us (9%)
  between operations  15.6 us (6%)
  local copies, waits for them, and re-layouts  7.93 us (3%)
  starting transfers between devices  3.91 us (2%)
    all_gather x2, waiting for transfers between devices, local(): piece = lax.all_gather(part, 'req', axis=0, tiled=True)  77.5 us
    psum x1, blocking collectives, local(): summed = lax.psum(onehot[:, None] * summary[None, :], 'req')  64.8 us
    dot_general x2, matrix products, chunk_stats(): lax.dot_general(normed, piece, (((1,), (1,)), ((), ())), preferred_elemen...  29.3 us
    ppermute x2, waiting for transfers between devices, local(): from_left = lax.ppermute(from_left, 'tensor', right)  21.6 us
    reduce_sum x1, other arithmetic, chunk_stats(): total = jnp.sum(expo, axis=1)  18 us
    all_gather x1, blocking collectives, local(): everyone = lax.all_gather(jnp.stack(mine), 'tensor', axis=0, tiled=False)  9.62 us
  transfers between devices with their start and end apart: 5, of which 4 were waited for; matrix products, arithmetic and copies ran while one was open for 8% of the time, Pallas kernels for 0%

profile of v1, /device:TPU:1, one launch (start us, length us, event | category | flops | bytes accessed | tf_op | source)
XLA Modules:
  0.0 251.8 jit_solution(1732280276588180706)
XLA Ops:
  7.2 1.7 slice.104
  9.0 1.0 slice.105
  10.0 0.8 concatenate.9
  10.8 0.7 reshape.148
  11.8 2.1 collective-permute-start
  13.9 1.3 collective-permute-start.1
  15.9 10.6 %collective-permute-done = bf16[1032,256]{1,0:T(8,128)(2,1)S(1)} collective-permute-done((bf16[1032,256]{1,0:T(8,128)(2,1)S(1)}, bf16[1032,256]{1,0:T(8,128)(2,1)S(1)}, u32[]{:S(2)}, u32[]{:S(2)}) %collective-permute-start) | collective-permute-done | bytes 528416 | tf_op jit(solution)/shard_map/ppermute | solution.py:51
  26.5 0.4 collective-permute-start.2
  27.7 1.1 constant_dynamic-update-slice_fusion.1
  28.8 11.0 %collective-permute-done.2 = bf16[1032,256]{1,0:T(8,128)(2,1)} collective-permute-done((bf16[1032,256]{1,0:T(8,128)(2,1)S(1)}, bf16[1032,256]{1,0:T(8,128)(2,1)}, u32[]{:S(2)}, u32[]{:S(2)}) %collective-permute-start.2) | collective-permute-done | bytes 528416 | tf_op jit(solution)/shard_map/ppermute | solution.py:51
  39.8 1.1 constant_dynamic-update-slice_fusion
  40.9 0.5 fusion.2
  41.4 31.3 %all-gather.5.cloned.1.call-done = bf16[4096,1024]{0,1:T(8,128)(2,1)} async-done(((bf16[128,1024]{0,1:T(8,128)(2,1)}), bf16[4096,1024]{0,1:T(8,128)(2,1)}) %all-gather.5.cloned.1.call-update) | async-done | bytes 8388624 | tf_op jit(solution)/shard_map/all_gather | solution.py:75
  72.8 14.6 %select_reduce_fusion.3 = (f32[1024]{0:T(1024)S(1)}, f32[1024,4096]{1,0:T(8,128)}) fusion(pred[4096]{0:T(1024)(128)(4,1)S(1)} %get-tuple-element.55, bf16[4096,1024]{0,1:T(8,128)(2,1)} %all-gather.5.cloned.1.call-done, f32[1024]{0:T(1024)S(1)} %bitcast.69, f32[1024]{0:T(1024)S(1)} %add_rsqrt_fusion, bf16[1032,1024]{1,0:T(8,128)(2,1)S(1)} %constant_dynamic-update-slice_fusion), kind=kOutput, calls=%fused_computation.9 | convolution fusion | flops 8602516480 | bytes 27279360 | tf_op jit(solution)/shard_map/dot_general | solution.py:12
  87.3 46.2 %all-gather.7.cloned.1.call-done = bf16[4096,1024]{0,1:T(8,128)(2,1)} async-done(((bf16[128,1024]{0,1:T(8,128)(2,1)}), bf16[4096,1024]{0,1:T(8,128)(2,1)}) %all-gather.7.cloned.1.call-update) | async-done | bytes 8388624 | tf_op jit(solution)/shard_map/all_gather | solution.py:75
  133.5 14.7 %select_reduce_fusion.2 = (f32[1024]{0:T(1024)S(1)}, f32[1024,4096]{1,0:T(8,128)}) fusion(pred[4096]{0:T(1024)(128)(4,1)S(1)} %get-tuple-element.56, bf16[4096,1024]{0,1:T(8,128)(2,1)} %all-gather.7.cloned.1.call-done, f32[1024]{0:T(1024)S(1)} %bitcast.70, f32[1024]{0:T(1024)S(1)} %add_rsqrt_fusion, bf16[1032,1024]{1,0:T(8,128)(2,1)S(1)} %constant_dynamic-update-slice_fusion), kind=kOutput, calls=%fused_computation.8 | convolution fusion | flops 8602516480 | bytes 27279360 | tf_op jit(solution)/shard_map/dot_general | solution.py:12
  148.3 18.0 %fusion = (f32[1024]{0:T(1024)S(1)}, f32[1024]{0:T(1024)S(1)}, f32[1024]{0:T(1024)S(1)}, f32[1024]{0:T(1024)S(1)}, f32[1024]{0:T(1024)S(1)}, /*index=5*/f32[1024]{0:T(1024)S(1)}) fusion(f32[1024,4096]{1,0:T(8,128)} %get-tuple-element.50, f32[1024]{0:T(1024)S(1)} %get-tuple-element.49, pred[4096]{0:T(1024)(128)(4,1)S(1)} %get-tuple-element.56, ...), kind=kLoop, calls=%fused_computation.5 | loop fusion | flops 67102720 | bytes 33632256 | tf_op jit(solution)/shard_map/reduce_sum | solution.py:18
  166.4 9.6 %all-gather.1 = f32[4,4,1024]{2,1,0:T(4,128)S(1)} all-gather(f32[1,4,1024]{2,1,0:T(4,128)S(1)} %maximum_bitcast_fusion), channel_id=2, replica_groups=mesh['req'=32,'tensor'=4] {'tensor'}, dimensions={0}, use_global_device_ids=true | all-gather | bytes 81920 | tf_op jit(solution)/shard_map/all_gather | solution.py:83
  176.2 0.6 fusion.33
  176.8 1.4 pad_maximum_fusion
  178.2 64.8 %psum.7 = f32[4,3]{0,1:T(4,128)S(1)} all-reduce(f32[4,3]{0,1:T(4,128)S(1)} %broadcast_multiply_fusion), channel_id=1, replica_groups=mesh['req'=32,'tensor'=4] {'req'}, use_global_device_ids=true, to_apply=%region_15.16 | all-reduce | flops 12 | bytes 96 | tf_op jit(solution)/shard_map/psum | solution.py:95
  243.1 0.6 slice_divide_fusion
  243.6 0.6 dynamic_slice.7
  244.3 0.6 dynamic_slice.6
  (36 shorter events, 0.9 us)
Async XLA Ops:
  7.2 4.5 %copy-start = (bf16[1024,256]{1,0:T(8,128)(2,1)S(1)}, bf16[1024,256]{1,0:T(8,128)(2,1)}, u32[]{:S(2)}) copy-start(bf16[1024,256]{1,0:T(8,128)(2,1)} %param.8) | copy-start | bytes 1572868
  7.2 65.6 %all-gather.5.cloned.1.call-start = ((), (), s32[]{:S(2)}) async-start(), calls=%async_computation | async-start | bytes 8650752 | tf_op jit(solution)/shard_map/all_gather | solution.py:75
  9.0 124.5 %all-gather.7.cloned.1.call-start = ((), (), s32[]{:S(2)}) async-start(), calls=%async_computation.1 | async-start | bytes 8650752 | tf_op jit(solution)/shard_map/all_gather | solution.py:75
  11.8 14.7 %collective-permute-start = (bf16[1032,256]{1,0:T(8,128)(2,1)S(1)}, bf16[1032,256]{1,0:T(8,128)(2,1)S(1)}, u32[]{:S(2)}, u32[]{:S(2)}) collective-permute-start(bf16[1032,256]{1,0:T(8,128)(2,1)S(1)} %get-tuple-element.29), channel_id=1, source_target_pairs={{0,1},{1,2},{2,3},{3,0},{4,5},{5,6},{6,7},{7,4},{8,9},{9,10},{10,1... | collective-permute-start | bytes 1585160 | tf_op jit(solution)/shard_map/ppermute | solution.py:51
  13.9 13.7 %collective-permute-start.1 = (bf16[1032,256]{1,0:T(8,128)(2,1)S(1)}, bf16[1032,256]{1,0:T(8,128)(2,1)}, u32[]{:S(2)}, u32[]{:S(2)}) collective-permute-start(bf16[1032,256]{1,0:T(8,128)(2,1)S(1)} %get-tuple-element.29), channel_id=1, source_target_pairs={{0,3},{1,0},{2,1},{3,2},{4,7},{5,4},{6,5},{7,6},{8,11},{9,8},{10,9... | collective-permute-start | bytes 1585160 | tf_op jit(solution)/shard_map/ppermute | solution.py:56
  26.5 13.3 %collective-permute-start.2 = (bf16[1032,256]{1,0:T(8,128)(2,1)S(1)}, bf16[1032,256]{1,0:T(8,128)(2,1)}, u32[]{:S(2)}, u32[]{:S(2)}) collective-permute-start(bf16[1032,256]{1,0:T(8,128)(2,1)S(1)} %collective-permute-done), channel_id=1, source_target_pairs={{0,1},{1,2},{2,3},{3,0},{4,5},{5,6},{6,7},{7,4},{8,9},{9,10},{10,1... | collective-permute-start | bytes 1585160 | tf_op jit(solution)/shard_map/ppermute | solution.py:51
  133.5 14.8 %slice-start = ((s8[16777216]{0:T(1024)(128)(4,1)}), s8[4194304]{0:T(1024)(128)(4,1)S(1)}, s32[]{:S(2)}) async-start(s8[16777216]{0:T(1024)(128)(4,1)} %bitcast.51), calls=%async_computation.2 | async-start | bytes 8388608
  133.5 14.8 %slice-start.1 = ((s8[16777216]{0:T(1024)(128)(4,1)}), s8[4194304]{0:T(1024)(128)(4,1)S(1)}, s32[]{:S(2)}) async-start(s8[16777216]{0:T(1024)(128)(4,1)} %bitcast.51), calls=%async_computation.3 | async-start | bytes 8388608
  133.5 14.8 %slice-start.2 = ((s8[16777216]{0:T(1024)(128)(4,1)}), s8[4194304]{0:T(1024)(128)(4,1)S(1)}, s32[]{:S(2)}) async-start(s8[16777216]{0:T(1024)(128)(4,1)} %bitcast.51), calls=%async_computation.4 | async-start | bytes 8388608
  133.5 14.8 %slice-start.3 = ((s8[16777216]{0:T(1024)(128)(4,1)}), s8[4194304]{0:T(1024)(128)(4,1)S(1)}, s32[]{:S(2)}) async-start(s8[16777216]{0:T(1024)(128)(4,1)} %bitcast.51), calls=%async_computation.5 | async-start | bytes 8388608
  133.5 14.8 %copy-start.1 = (s32[1024]{0:T(1024)S(1)}, s32[1024]{0:T(1024)}, u32[]{:S(2)}) copy-start(s32[1024]{0:T(1024)} %param.11) | copy-start | bytes 12292
Sparse Core Ops, SparseCore 0:
  10.2 62.5 all-gather.4
  74.9 58.5 all-gather.6
